TPU v7x, 128 devices: a whole 4x4x4 slice. The times are simulated.
128 devices in a mesh: group: 16 (over z, y), inner: 8 (over x, core).
Axes of the slice: x: 4, y: 4, z: 4, core: 2. Of those that a mesh axis runs over, the one named last changes fastest.
Arguments:
- tokens: bfloat16 [16384, 7168], P(('group', 'inner')), may hold values from -6 to 6
- target: int32 [16384], P(('group', 'inner')), may hold values from 0 to 16, as said below
- gate_scale: float32 [16384], P(('group', 'inner')), may hold values from 0.25 to 2.5
- gate_weight: bfloat16 [16, 7168, 2048], P('group', None, 'inner'), may hold values from -0.0625 to 0.0625
- up_weight: bfloat16 [16, 7168, 2048], P('group', None, 'inner'), may hold values from -0.0625 to 0.0625
- down_weight: bfloat16 [16, 2048, 7168], P('group', 'inner'), may hold values from -0.125 to 0.125
Outputs:
- routed_out: bfloat16 [16384, 7168], P(('group', 'inner'))
Inputs may be any that keep to these rules, and one draw needn't show every extreme that they name: 16 means that the token uses no expert of this round. Among the 128 tokens of one device at most 10 target any one group, and in every device some group is targeted by exactly 10 of them.
All inputs are finite; a program needn't handle non-finite values.
Results may differ from a plain program's by a relative error of at most 0.0095.
Values may be sent and summed in bfloat16 or wider, within the bound.
A program may use at most 192 MiB of HBM per device.

v0:
```python
import jax
import jax.numpy as jnp
from jax import lax
from jax.sharding import PartitionSpec as P


def expert_part(rows_in, gate_mat, up_mat, down_mat):
    gate_pre = jnp.dot(rows_in, gate_mat, preferred_element_type=jnp.float32)
    up_pre = jnp.dot(rows_in, up_mat, preferred_element_type=jnp.float32)
    hidden = (jax.nn.silu(gate_pre) * up_pre).astype(jnp.bfloat16)
    return jnp.dot(hidden, down_mat, preferred_element_type=jnp.float32)


def body(tokens, target, gate_scale, gate_weight, up_weight, down_weight):
    groups = lax.axis_size("group")
    inner_size = lax.axis_size("inner")
    tok_count = tokens.shape[0]
    model_width = tokens.shape[1]
    capacity = tok_count * 5 // (4 * groups)
    slot_count = groups * capacity
    onehot = (target[:, None] == jnp.arange(groups, dtype=jnp.int32)[None, :]).astype(jnp.int32)
    rank_in = jnp.sum((jnp.cumsum(onehot, axis=0) - onehot) * onehot, axis=1)
    slot_of = jnp.where(target < groups, target * capacity + rank_in, slot_count)
    dispatch = (slot_of[None, :] == jnp.arange(slot_count, dtype=jnp.int32)[:, None]).astype(
        jnp.bfloat16
    )
    outbound = jnp.dot(dispatch, tokens, preferred_element_type=jnp.float32).astype(jnp.bfloat16)
    outbound = outbound.reshape(groups, capacity, model_width)
    received = lax.all_to_all(outbound, "group", 0, 0, tiled=True)
    gathered = lax.all_gather(received, "inner", axis=0, tiled=False)
    partial_value = expert_part(
        gathered.reshape(-1, model_width), gate_weight[0], up_weight[0], down_weight[0]
    )
    partial_value = partial_value.astype(jnp.bfloat16).reshape(
        inner_size, groups, capacity, model_width
    )
    pieces = lax.all_to_all(partial_value, "inner", 0, 0, tiled=True)
    summed = jnp.sum(pieces.astype(jnp.float32), axis=0).astype(jnp.bfloat16)
    back_rows = lax.all_to_all(summed, "group", 0, 0, tiled=True).reshape(slot_count, model_width)
    expert_out = lax.dot_general(
        dispatch, back_rows, (((0,), (0,)), ((), ())), preferred_element_type=jnp.float32
    )
    return (gate_scale[:, None] * expert_out).astype(jnp.bfloat16)


def solution(mesh):
    in_specs = (
        P(("group", "inner"), None),
        P(("group", "inner")),
        P(("group", "inner")),
        P("group", None, "inner"),
        P("group", None, "inner"),
        P("group", "inner", None),
    )
    out_specs = P(("group", "inner"), None)
    return jax.shard_map(body, mesh=mesh, in_specs=in_specs, out_specs=out_specs, check_vma=False)
```

profile of v0, /device:TPU:0, one launch (start us, length us, event | category | flops | bytes accessed | tf_op | source)
XLA Modules:
  0.0 581.5 jit_solution(12582657928746278648)
XLA Ops:
  6.5 0.0 copy-start
  6.5 0.0 all-gather.3.cloned.1.call-start
  6.5 0.9 fusion.18
  7.4 0.2 reduce_window_sum.11
  7.6 0.8 select_reduce_fusion
  8.4 0.7 compare_select_fusion
  9.1 0.0 copy-done
  9.1 2.1 convolution_convert_fusion.1
  11.2 4.5 reshape.15
  15.7 53.4 %all_to_all.15 = bf16[16,10,7168]{2,1,0:T(8,128)(2,1)S(1)} all-to-all(bf16[16,10,7168]{2,1,0:T(8,128)(2,1)} %reshape.15), channel_id=1, replica_groups=mesh['group'=16,'inner'=8] {'group'}, dimensions={0} | all-to-all | bytes 4587520 | tf_op jit(solution)/shard_map/all_to_all | solution.py:29
  69.1 2.6 copy.14
  71.7 0.0 all-gather.3.cloned.1.call-update
  71.7 89.1 %all-gather.3.cloned.1.call-done = bf16[128,10,7168]{2,0,1:T(8,128)(2,1)} async-done(((bf16[16,10,7168]{2,0,1:T(8,128)(2,1)}), bf16[128,10,7168]{2,0,1:T(8,128)(2,1)}) %all-gather.3.cloned.1.call-update) | async-done | bytes 18350096 | tf_op jit(solution)/shard_map/all_gather | solution.py:30
  160.9 21.5 %copy.15 = bf16[128,10,7168]{2,1,0:T(8,128)(2,1)} copy(bf16[128,10,7168]{2,0,1:T(8,128)(2,1)} %all-gather.3.cloned.1.call-done) | data formatting | bytes 36700160 | tf_op jit(solution)/shard_map/all_gather | solution.py:30
  182.4 28.2 %reshape.16 = bf16[1280,7168]{1,0:T(8,128)(2,1)} reshape(bf16[128,10,7168]{2,1,0:T(8,128)(2,1)} %copy.15) | data formatting | bytes 36700160 | tf_op jit(solution)/shard_map/reshape | solution.py:32
  210.6 9.8 %fusion.4 = f32[1280,256]{1,0:T(8,128)S(1)} fusion(bf16[1280,7168]{1,0:T(8,128)(2,1)} %reshape.16, bf16[1,7168,256]{2,1,0:T(8,128)(2,1)} %param.9), kind=kOutput, calls=%fused_computation.7 | convolution fusion | flops 4697620480 | bytes 23330816 | tf_op jit(solution)/shard_map/dot_general | solution.py:8
  220.4 27.1 %convolution_convert_fusion = bf16[1280,7168]{1,0:T(8,128)(2,1)} fusion(bf16[1,256,7168]{2,1,0:T(8,128)(2,1)} %param.11, bf16[1280,7168]{1,0:T(8,128)(2,1)} %reshape.16, bf16[1,7168,256]{2,1,0:T(8,128)(2,1)} %param.10, f32[1280,256]{1,0:T(8,128)S(1)} %fusion.4), kind=kOutput, calls=%fused_computation | convolution fusion | flops 9406382080 | bytes 45350912 | tf_op jit(solution)/shard_map/dot_general | solution.py:11
  247.6 27.7 %reshape.17 = bf16[8,16,10,7168]{3,2,1,0:T(8,128)(2,1)} reshape(bf16[1280,7168]{1,0:T(8,128)(2,1)} %convolution_convert_fusion) | data formatting | bytes 36700160 | tf_op jit(solution)/shard_map/reshape | solution.py:34
  275.2 17.2 %copy.16 = bf16[8,16,10,7168]{3,1,2,0:T(8,128)(2,1)S(1)} copy(bf16[8,16,10,7168]{3,2,1,0:T(8,128)(2,1)} %reshape.17) | data formatting | bytes 36700160 | tf_op jit(solution)/shard_map/reshape | solution.py:34
  292.4 208.1 %all_to_all.16 = bf16[8,16,10,7168]{3,1,2,0:T(8,128)(2,1)} all-to-all(bf16[8,16,10,7168]{3,1,2,0:T(8,128)(2,1)S(1)} %copy.16), channel_id=1, replica_groups=mesh['group'=16,'inner'=8] {'inner'}, dimensions={0} | all-to-all | bytes 36700160 | tf_op jit(solution)/shard_map/all_to_all | solution.py:37
  500.6 11.1 %reduce_sum.22 = bf16[16,10,7168]{2,0,1:T(8,128)(2,1)} reduce(bf16[8,16,10,7168]{3,1,2,0:T(8,128)(2,1)} %all_to_all.16, bf16[]{:T(256)} %constant.17.clone.1), dimensions={0}, to_apply=%region_2.3 | reduce | flops 8028160 | bytes 20643842 | tf_op jit(solution)/shard_map/reduce_sum | solution.py:38
  511.6 3.0 copy.17
  514.7 0.0 copy-start.1
  514.7 51.9 %all_to_all.17 = bf16[16,10,7168]{2,1,0:T(8,128)(2,1)} all-to-all(bf16[16,10,7168]{2,1,0:T(8,128)(2,1)S(1)} %copy.17), channel_id=1, replica_groups=mesh['group'=16,'inner'=8] {'group'}, dimensions={0} | all-to-all | bytes 4587520 | tf_op jit(solution)/shard_map/all_to_all | solution.py:39
  566.6 0.0 copy-start.2
  566.6 4.5 reshape.18
  571.1 0.0 copy-done.2
  571.1 3.6 fusion
  574.7 0.0 copy-done.1
Async XLA Ops:
  6.5 2.6 copy-start
  6.5 154.3 %all-gather.3.cloned.1.call-start = ((), (), s32[]{:S(2)}) async-start(), calls=%async_computation.3 | async-start | bytes 20643840 | tf_op jit(solution)/shard_map/all_gather | solution.py:30
  514.7 60.0 %copy-start.1 = (bf16[128,7168]{1,0:T(8,128)(2,1)S(1)}, bf16[128,7168]{1,0:T(8,128)(2,1)}, u32[]{:S(2)}) copy-start(bf16[128,7168]{1,0:T(8,128)(2,1)} %param.6) | copy-start | bytes 5505028
  566.6 4.5 copy-start.2
Sparse Core Ops, SparseCore 0:
  71.9 88.9 all-gather.2
where the time goes:
time: 584 us; the launch traced here: 582 us
  blocking collectives  313 us (54%)
  local copies, waits for them, and re-layouts  109 us (19%)
  waiting for transfers between devices  89.2 us (15%)
  matrix products  42.7 us (7%)
  other arithmetic  13.6 us (2%)
  between operations  13.4 us (2%)
    all_to_all x1, blocking collectives, body(): pieces = lax.all_to_all(partial_value, 'inner', 0, 0, tiled=True)  208 us
    all_gather x1, waiting for transfers between devices, body(): gathered = lax.all_gather(received, 'inner', axis=0, tiled=False)  89.1 us
    all_to_all x1, blocking collectives, body(): received = lax.all_to_all(outbound, 'group', 0, 0, tiled=True)  53.4 us
    all_to_all x1, blocking collectives, body(): lax.all_to_all(summed, 'group', 0, 0, tiled=True)  51.9 us
    reshape x2, local copies, waits for them, and re-layouts, body(): partial_value.astype(jnp.bfloat16)  44.8 us
    reshape x1, local copies, waits for them, and re-layouts, body(): gathered.reshape(-1, model_width)  28.2 us
    dot_general x1, matrix products, expert_part(): return jnp.dot(hidden, down_mat, preferred_element_type=jnp.float32)  27.1 us
    all_gather x1, local copies, waits for them, and re-layouts, body(): gathered = lax.all_gather(received, 'inner', axis=0, tiled=False)  21.5 us
  transfers between devices with their start and end apart: 1, of which 1 were waited for; matrix products, arithmetic and copies ran while one was open for 0% of the time, Pallas kernels for 0%

commit v1 on v0

--- a/solution.py
+++ b/solution.py
@@ -26,7 +26,19 @@
     )
     outbound = jnp.dot(dispatch, tokens, preferred_element_type=jnp.float32).astype(jnp.bfloat16)
     outbound = outbound.reshape(groups, capacity, model_width)
-    received = lax.all_to_all(outbound, "group", 0, 0, tiled=True)
+    ways, here = (lax.axis_size("group"), lax.axis_index("group"))
+    width = outbound.shape[0] // ways
+    shape = list(outbound.shape)
+    shape[0] = width
+    height = shape[0]
+    shape[0] = height * ways
+    full = jnp.zeros(shape, outbound.dtype)
+    for mask in range(ways):
+        part = lax.dynamic_slice_in_dim(outbound, (here ^ mask) * width, width, axis=0)
+        if mask:
+            part = lax.ppermute(part, "group", [(d, d ^ mask) for d in range(ways)])
+        full = lax.dynamic_update_slice_in_dim(full, part, (here ^ mask) * height, axis=0)
+    received = full
     gathered = lax.all_gather(received, "inner", axis=0, tiled=False)
     partial_value = expert_part(
         gathered.reshape(-1, model_width), gate_weight[0], up_weight[0], down_weight[0]

time: 584 us -> 686 us (1.17)
  local copies, waits for them, and re-layouts: 109 us -> 193 us
  blocking collectives: 313 us -> 260 us
  waiting for transfers between devices: 89.2 us -> 129 us
  starting transfers between devices: 0.01 us -> 30.1 us
    dynamic_update_slice x0 -> x16, local copies, waits for them, and re-layouts: none -> 70.9 us  [body(): lax.dynamic_update_slice_in_dim(full, part, (here ^ mask) * height, axis=0)]
    all_to_all x1 -> x0, blocking collectives: 53.4 us -> none  [body(): received = lax.all_to_all(outbound, 'group', 0, 0, tiled=True)]
    ppermute x0 -> x15, waiting for transfers between devices: none -> 37.6 us  [body(): part = lax.ppermute(part, 'group', [(d, d ^ mask) for d in range(ways)])]
    ppermute x0 -> x15, starting transfers between devices: none -> 30.1 us  [body(): part = lax.ppermute(part, 'group', [(d, d ^ mask) for d in range(ways)])]
    all_gather x1 -> x18, local copies, waits for them, and re-layouts: 21.5 us -> 32.6 us  [body(): gathered = lax.all_gather(received, 'inner', axis=0, tiled=False)]
  transfers between devices with their start and end apart: 1 -> 16, of which waited for: 1 -> 5; matrix products, arithmetic and copies ran while one was open for 0% -> 2% of each run, Pallas kernels for 0% -> 0%
where the time goes in v1:
time: 686 us; the launch traced here: 682 us
  blocking collectives  260 us (38%)
  local copies, waits for them, and re-layouts  193 us (28%)
  waiting for transfers between devices  129 us (19%)
  matrix products  42.9 us (6%)
  starting transfers between devices  30.1 us (4%)
  other arithmetic  13.6 us (2%)
  between operations  13.6 us (2%)
    all_to_all x1, blocking collectives, body(): pieces = lax.all_to_all(partial_value, 'inner', 0, 0, tiled=True)  208 us
    all_gather x1, waiting for transfers between devices, body(): gathered = lax.all_gather(received, 'inner', axis=0, tiled=False)  91.9 us
    dynamic_update_slice x16, local copies, waits for them, and re-layouts, body(): lax.dynamic_update_slice_in_dim(full, part, (here ^ mask) * height, axis=0)  70.9 us
    all_to_all x1, blocking collectives, body(): lax.all_to_all(summed, 'group', 0, 0, tiled=True)  51.8 us
    reshape x2, local copies, waits for them, and re-layouts, body(): partial_value.astype(jnp.bfloat16)  44.9 us
    ppermute x15, waiting for transfers between devices, body(): part = lax.ppermute(part, 'group', [(d, d ^ mask) for d in range(ways)])  37.6 us
    all_gather x18, local copies, waits for them, and re-layouts, body(): gathered = lax.all_gather(received, 'inner', axis=0, tiled=False)  32.6 us
    ppermute x15, starting transfers between devices, body(): part = lax.ppermute(part, 'group', [(d, d ^ mask) for d in range(ways)])  30.1 us
  transfers between devices with their start and end apart: 16, of which 5 were waited for; matrix products, arithmetic and copies ran while one was open for 2% of the time, Pallas kernels for 0%

profile of v1, /device:TPU:0, one launch (start us, length us, event | category | flops | bytes accessed | tf_op | source)
XLA Modules:
  0.0 682.1 jit_solution(16055085075931606024)
XLA Ops:
  11.8 4.5 reshape.47
  19.6 6.6 collective-permute-start.14
  32.4 6.4 collective-permute-done.14
  48.2 18.1 %collective-permute-done.11 = bf16[1,10,7168]{2,1,0:T(8,128)(2,1)S(1)} collective-permute-done((bf16[1,10,7168]{2,1,0:T(8,128)(2,1)S(1)}, bf16[1,10,7168]{2,1,0:T(8,128)(2,1)S(1)}, u32[]{:S(2)}, u32[]{:S(2)}) %collective-permute-start.11) | collective-permute-done | bytes 143392 | tf_op jit(solution)/shard_map/ppermute | solution.py:39
  74.5 10.5 %collective-permute-done.6 = bf16[1,10,7168]{2,1,0:T(8,128)(2,1)S(1)} collective-permute-done((bf16[1,10,7168]{2,1,0:T(8,128)(2,1)S(1)}, bf16[1,10,7168]{2,1,0:T(8,128)(2,1)S(1)}, u32[]{:S(2)}, u32[]{:S(2)}) %collective-permute-start.6) | collective-permute-done | bytes 143392 | tf_op jit(solution)/shard_map/ppermute | solution.py:39
  89.1 4.4 dynamic_update_slice.64
  102.9 4.4 dynamic_update_slice.65
  107.3 4.4 dynamic_update_slice.66
  111.8 4.4 dynamic_update_slice.67
  116.2 4.4 dynamic_update_slice.68
  120.7 4.4 dynamic_update_slice.69
  125.1 4.4 dynamic_update_slice.70
  129.5 4.4 dynamic_update_slice.71
  134.0 4.4 dynamic_update_slice.72
  138.4 4.4 dynamic_update_slice.73
  142.8 4.4 dynamic_update_slice.74
  147.2 4.4 dynamic_update_slice.75
  151.7 4.4 dynamic_update_slice.76
  156.1 4.4 dynamic_update_slice.77
  160.5 4.4 dynamic_update_slice.78
  165.0 4.4 dynamic_update_slice.79
  169.4 91.9 %all-gather.2.cloned.1.call-done = bf16[8,16,10,7168]{3,1,2,0:T(8,128)(2,1)} async-done(((bf16[1,16,10,7168]{3,1,2,0:T(8,128)(2,1)}), bf16[8,16,10,7168]{3,1,2,0:T(8,128)(2,1)}) %all-gather.2.cloned.1.call-update) | async-done | bytes 18350096 | tf_op jit(solution)/shard_map/all_gather | solution.py:42
  261.3 21.5 %copy.77 = bf16[8,16,10,7168]{3,2,1,0:T(8,128)(2,1)} copy(bf16[8,16,10,7168]{3,1,2,0:T(8,128)(2,1)} %all-gather.2.cloned.1.call-done) | data formatting | bytes 36700160 | tf_op jit(solution)/shard_map/all_gather | solution.py:42
  282.7 28.3 %reshape.48 = bf16[1280,7168]{1,0:T(8,128)(2,1)} reshape(bf16[8,16,10,7168]{3,2,1,0:T(8,128)(2,1)} %copy.77) | data formatting | bytes 36700160 | tf_op jit(solution)/shard_map/reshape | solution.py:44
  311.0 9.8 %fusion.4 = f32[1280,256]{1,0:T(8,128)S(1)} fusion(bf16[1280,7168]{1,0:T(8,128)(2,1)} %reshape.48, bf16[1,7168,256]{2,1,0:T(8,128)(2,1)} %param.9), kind=kOutput, calls=%fused_computation.7 | convolution fusion | flops 4697620480 | bytes 23330816 | tf_op jit(solution)/shard_map/dot_general | solution.py:8
  320.8 27.4 %convolution_convert_fusion = bf16[1280,7168]{1,0:T(8,128)(2,1)} fusion(bf16[1,256,7168]{2,1,0:T(8,128)(2,1)} %param.11, bf16[1280,7168]{1,0:T(8,128)(2,1)} %reshape.48, bf16[1,7168,256]{2,1,0:T(8,128)(2,1)} %param.10, f32[1280,256]{1,0:T(8,128)S(1)} %fusion.4), kind=kOutput, calls=%fused_computation | convolution fusion | flops 9406382080 | bytes 45350912 | tf_op jit(solution)/shard_map/dot_general | solution.py:11
  348.2 27.7 %reshape.49 = bf16[8,16,10,7168]{3,2,1,0:T(8,128)(2,1)} reshape(bf16[1280,7168]{1,0:T(8,128)(2,1)} %convolution_convert_fusion) | data formatting | bytes 36700160 | tf_op jit(solution)/shard_map/reshape | solution.py:46
  375.9 17.2 %copy.78 = bf16[8,16,10,7168]{3,1,2,0:T(8,128)(2,1)S(1)} copy(bf16[8,16,10,7168]{3,2,1,0:T(8,128)(2,1)} %reshape.49) | data formatting | bytes 36700160 | tf_op jit(solution)/shard_map/reshape | solution.py:46
  393.1 208.2 %all_to_all.10 = bf16[8,16,10,7168]{3,1,2,0:T(8,128)(2,1)} all-to-all(bf16[8,16,10,7168]{3,1,2,0:T(8,128)(2,1)S(1)} %copy.78), channel_id=1, replica_groups=mesh['group'=16,'inner'=8] {'inner'}, dimensions={0} | all-to-all | bytes 36700160 | tf_op jit(solution)/shard_map/all_to_all | solution.py:49
  601.3 11.0 %reduce_sum.22 = bf16[16,10,7168]{2,0,1:T(8,128)(2,1)} reduce(bf16[8,16,10,7168]{3,1,2,0:T(8,128)(2,1)} %all_to_all.10, bf16[]{:T(256)} %constant.53.clone.1), dimensions={0}, to_apply=%region_2.3 | reduce | flops 8028160 | bytes 20643842 | tf_op jit(solution)/shard_map/reduce_sum | solution.py:50
  615.3 51.8 %all_to_all.11 = bf16[16,10,7168]{2,1,0:T(8,128)(2,1)} all-to-all(bf16[16,10,7168]{2,1,0:T(8,128)(2,1)S(1)} %copy.79), channel_id=1, replica_groups=mesh['group'=16,'inner'=8] {'group'}, dimensions={0} | all-to-all | bytes 4587520 | tf_op jit(solution)/shard_map/all_to_all | solution.py:51
  667.1 4.6 reshape.50
  (63 shorter events, 52.3 us)
Async XLA Ops:
  6.5 3.1 copy-start
  6.5 254.7 %all-gather.2.cloned.1.call-start = ((), (), s32[]{:S(2)}) async-start(), calls=%async_computation.2 | async-start | bytes 20643840 | tf_op jit(solution)/shard_map/all_gather | solution.py:42
  9.1 0.6 copy-start.2
  19.6 19.3 %collective-permute-start.14 = (bf16[1,10,7168]{2,1,0:T(8,128)(2,1)S(1)}, bf16[1,10,7168]{2,1,0:T(8,128)(2,1)S(1)}, u32[]{:S(2)}, u32[]{:S(2)}) collective-permute-start(bf16[1,10,7168]{2,1,0:T(8,128)(2,1)S(1)} %get-tuple-element.5), channel_id=1, source_target_pairs={{0,120},{8,112},{16,104},{24,96},{32,88},{40,80},{48,72},{56,64},{... | collective-permute-start | bytes 430088 | tf_op jit(solution)/shard_map/ppermute | solution.py:39
  26.1 17.1 %collective-permute-start.13 = (bf16[1,10,7168]{2,1,0:T(8,128)(2,1)S(1)}, bf16[1,10,7168]{2,1,0:T(8,128)(2,1)S(1)}, u32[]{:S(2)}, u32[]{:S(2)}) collective-permute-start(bf16[1,10,7168]{2,1,0:T(8,128)(2,1)S(1)} %get-tuple-element.6), channel_id=1, source_target_pairs={{0,112},{8,120},{16,96},{24,104},{32,80},{40,88},{48,64},{56,72},{... | collective-permute-start | bytes 430088 | tf_op jit(solution)/shard_map/ppermute | solution.py:39
  26.4 20.1 %collective-permute-start.12 = (bf16[1,10,7168]{2,1,0:T(8,128)(2,1)S(1)}, bf16[1,10,7168]{2,1,0:T(8,128)(2,1)S(1)}, u32[]{:S(2)}, u32[]{:S(2)}) collective-permute-start(bf16[1,10,7168]{2,1,0:T(8,128)(2,1)S(1)} %get-tuple-element.7), channel_id=1, source_target_pairs={{0,104},{8,96},{16,120},{24,112},{32,72},{40,64},{48,88},{56,80},{... | collective-permute-start | bytes 430088 | tf_op jit(solution)/shard_map/ppermute | solution.py:39
  29.3 37.0 %collective-permute-start.11 = (bf16[1,10,7168]{2,1,0:T(8,128)(2,1)S(1)}, bf16[1,10,7168]{2,1,0:T(8,128)(2,1)S(1)}, u32[]{:S(2)}, u32[]{:S(2)}) collective-permute-start(bf16[1,10,7168]{2,1,0:T(8,128)(2,1)S(1)} %get-tuple-element.8), channel_id=1, source_target_pairs={{0,96},{8,104},{16,112},{24,120},{32,64},{40,72},{48,80},{56,88},{... | collective-permute-start | bytes 430088 | tf_op jit(solution)/shard_map/ppermute | solution.py:39
  29.7 38.1 %collective-permute-start.10 = (bf16[1,10,7168]{2,1,0:T(8,128)(2,1)S(1)}, bf16[1,10,7168]{2,1,0:T(8,128)(2,1)S(1)}, u32[]{:S(2)}, u32[]{:S(2)}) collective-permute-start(bf16[1,10,7168]{2,1,0:T(8,128)(2,1)S(1)} %get-tuple-element.9), channel_id=1, source_target_pairs={{0,88},{8,80},{16,72},{24,64},{32,120},{40,112},{48,104},{56,96},{... | collective-permute-start | bytes 430088 | tf_op jit(solution)/shard_map/ppermute | solution.py:39
  38.9 30.6 %collective-permute-start.9 = (bf16[1,10,7168]{2,1,0:T(8,128)(2,1)S(1)}, bf16[1,10,7168]{2,1,0:T(8,128)(2,1)S(1)}, u32[]{:S(2)}, u32[]{:S(2)}) collective-permute-start(bf16[1,10,7168]{2,1,0:T(8,128)(2,1)S(1)} %get-tuple-element.10), channel_id=1, source_target_pairs={{0,80},{8,88},{16,64},{24,72},{32,112},{40,120},{48,96},{56,104},{... | collective-permute-start | bytes 430088 | tf_op jit(solution)/shard_map/ppermute | solution.py:39
  43.2 27.2 %collective-permute-start.8 = (bf16[1,10,7168]{2,1,0:T(8,128)(2,1)S(1)}, bf16[1,10,7168]{2,1,0:T(8,128)(2,1)S(1)}, u32[]{:S(2)}, u32[]{:S(2)}) collective-permute-start(bf16[1,10,7168]{2,1,0:T(8,128)(2,1)S(1)} %get-tuple-element.11), channel_id=1, source_target_pairs={{0,72},{8,64},{16,88},{24,80},{32,104},{40,96},{48,120},{56,112},{... | collective-permute-start | bytes 430088 | tf_op jit(solution)/shard_map/ppermute | solution.py:39
  46.5 26.3 %collective-permute-start.7 = (bf16[1,10,7168]{2,1,0:T(8,128)(2,1)S(1)}, bf16[1,10,7168]{2,1,0:T(8,128)(2,1)S(1)}, u32[]{:S(2)}, u32[]{:S(2)}) collective-permute-start(bf16[1,10,7168]{2,1,0:T(8,128)(2,1)S(1)} %get-tuple-element.12), channel_id=1, source_target_pairs={{0,64},{8,72},{16,80},{24,88},{32,96},{40,104},{48,112},{56,120},{... | collective-permute-start | bytes 430088 | tf_op jit(solution)/shard_map/ppermute | solution.py:39
  66.3 18.8 %collective-permute-start.6 = (bf16[1,10,7168]{2,1,0:T(8,128)(2,1)S(1)}, bf16[1,10,7168]{2,1,0:T(8,128)(2,1)S(1)}, u32[]{:S(2)}, u32[]{:S(2)}) collective-permute-start(bf16[1,10,7168]{2,1,0:T(8,128)(2,1)S(1)} %get-tuple-element.13), channel_id=1, source_target_pairs={{0,56},{8,48},{16,40},{24,32},{32,24},{40,16},{48,8},{56,0},{64,12... | collective-permute-start | bytes 430088 | tf_op jit(solution)/shard_map/ppermute | solution.py:39
  67.9 17.2 %collective-permute-start.5 = (bf16[1,10,7168]{2,1,0:T(8,128)(2,1)S(1)}, bf16[1,10,7168]{2,1,0:T(8,128)(2,1)S(1)}, u32[]{:S(2)}, u32[]{:S(2)}) collective-permute-start(bf16[1,10,7168]{2,1,0:T(8,128)(2,1)S(1)} %get-tuple-element.14), channel_id=1, source_target_pairs={{0,48},{8,56},{16,32},{24,40},{32,16},{40,24},{48,0},{56,8},{64,11... | collective-permute-start | bytes 430088 | tf_op jit(solution)/shard_map/ppermute | solution.py:39
  69.4 26.4 %collective-permute-start.4 = (bf16[1,10,7168]{2,1,0:T(8,128)(2,1)}, bf16[1,10,7168]{2,1,0:T(8,128)(2,1)S(1)}, u32[]{:S(2)}, u32[]{:S(2)}) collective-permute-start(bf16[1,10,7168]{2,1,0:T(8,128)(2,1)} %get-tuple-element.15), channel_id=1, source_target_pairs={{0,40},{8,32},{16,56},{24,48},{32,8},{40,0},{48,24},{56,16},{64,10... | collective-permute-start | bytes 430088 | tf_op jit(solution)/shard_map/ppermute | solution.py:39
  70.4 25.7 %collective-permute-start.3 = (bf16[1,10,7168]{2,1,0:T(8,128)(2,1)}, bf16[1,10,7168]{2,1,0:T(8,128)(2,1)}, u32[]{:S(2)}, u32[]{:S(2)}) collective-permute-start(bf16[1,10,7168]{2,1,0:T(8,128)(2,1)} %get-tuple-element.16), channel_id=1, source_target_pairs={{0,32},{8,40},{16,48},{24,56},{32,0},{40,8},{48,16},{56,24},{64,96... | collective-permute-start | bytes 430088 | tf_op jit(solution)/shard_map/ppermute | solution.py:39
  72.8 24.5 %collective-permute-start.2 = (bf16[1,10,7168]{2,1,0:T(8,128)(2,1)}, bf16[1,10,7168]{2,1,0:T(8,128)(2,1)}, u32[]{:S(2)}, u32[]{:S(2)}) collective-permute-start(bf16[1,10,7168]{2,1,0:T(8,128)(2,1)} %get-tuple-element.17), channel_id=1, source_target_pairs={{0,24},{8,16},{16,8},{24,0},{32,56},{40,48},{48,40},{56,32},{64,88... | collective-permute-start | bytes 430088 | tf_op jit(solution)/shard_map/ppermute | solution.py:39
  85.1 14.1 %collective-permute-start.1 = (bf16[1,10,7168]{2,1,0:T(8,128)(2,1)}, bf16[1,10,7168]{2,1,0:T(8,128)(2,1)}, u32[]{:S(2)}, u32[]{:S(2)}) collective-permute-start(bf16[1,10,7168]{2,1,0:T(8,128)(2,1)} %get-tuple-element.18), channel_id=1, source_target_pairs={{0,16},{8,24},{16,0},{24,8},{32,48},{40,56},{48,32},{56,40},{64,80... | collective-permute-start | bytes 430088 | tf_op jit(solution)/shard_map/ppermute | solution.py:39
  85.1 15.9 %collective-permute-start = (bf16[1,10,7168]{2,1,0:T(8,128)(2,1)}, bf16[1,10,7168]{2,1,0:T(8,128)(2,1)}, u32[]{:S(2)}, u32[]{:S(2)}) collective-permute-start(bf16[1,10,7168]{2,1,0:T(8,128)(2,1)} %get-tuple-element.19), channel_id=1, source_target_pairs={{0,8},{8,0},{16,24},{24,16},{32,40},{40,32},{48,56},{56,48},{64,72... | collective-permute-start | bytes 430088 | tf_op jit(solution)/shard_map/ppermute | solution.py:39
  667.1 4.6 copy-start.3
  667.1 4.6 copy-start.4
  667.1 8.2 %copy-start.1 = (bf16[128,7168]{1,0:T(8,128)(2,1)S(1)}, bf16[128,7168]{1,0:T(8,128)(2,1)}, u32[]{:S(2)}) copy-start(bf16[128,7168]{1,0:T(8,128)(2,1)} %param.6) | copy-start | bytes 5505028
Sparse Core Ops, SparseCore 0:
  169.5 91.6 all-gather.1
